TPU v7x, 512 devices: a whole 4x8x8 slice. The times are simulated.
512 devices in a mesh: ctx: 64 (over z, y), tp: 4 (over x), dp: 2 (over core).
Axes of the slice: x: 4, y: 8, z: 8, core: 2. Of those that a mesh axis runs over, the one named last changes fastest.
Arguments:
- projected: bfloat16 [3, 2, 16384, 1024], P(None, 'dp', 'ctx', 'tp'), may hold values from -6 to 6
- segment_ids: int32 [2, 16384], P('dp', 'ctx'), may hold values from 0 to 31, never falling along the last dimension, each value on 1 to 768 neighbouring positions
- short_filter: float32 [3, 3, 1024], P(None, None, 'tp'), may hold values from -3.5 to 3.5
- long_filter: float32 [64, 16384], P('tp', 'ctx'), may hold values from -4 to 4
- out_proj: bfloat16 [1024, 1024], P('tp'), may hold values from -0.1875 to 0.1875
- mixed_cotangent: bfloat16 [2, 16384, 1024], P('dp', 'ctx', 'tp'), may hold values from -6 to 6
Outputs:
- mixed: bfloat16 [2, 16384, 1024], P('dp', 'ctx', 'tp')
- grad_projected: bfloat16 [3, 2, 16384, 1024], P(None, 'dp', 'ctx', 'tp')
- grad_short: float32 [3, 3, 1024], P(None, None, 'tp')
- grad_long: float32 [64, 16384], P('tp', 'ctx')
- grad_out_proj: float32 [1024, 1024], P('tp')
Inputs may be any that keep to these rules, and one draw needn't show every extreme that they name: `segment_ids`: along each window the id never falls; every id covers 1 to 768 consecutive positions, and one covers exactly 768.
All inputs are finite; a program needn't handle non-finite values.
Results may differ from a plain program's by a relative error of at most 0.0049.
Values may be sent and summed in bfloat16 or wider, within the bound.
A program may use at most 64 MiB of HBM per device.

v0:
```python
import math
import jax
import jax.numpy as jnp
from jax import lax
from jax.sharding import PartitionSpec as P

highest_precision = lax.Precision.HIGHEST


def shifted(value, axis, steps):
    count = lax.axis_size(axis)
    first, last = (max(0, -steps), min(count, count - steps))
    return lax.ppermute(value, axis, [(source, source + steps) for source in range(first, last)])


def angle_table(height, breadth, period, direction):
    product = (
        jnp.arange(height, dtype=jnp.int32)[:, None]
        * jnp.arange(breadth, dtype=jnp.int32)[None, :]
        % period
    )
    angles = direction * 2.0 * math.pi / period * product.astype(jnp.float32)
    return (jnp.cos(angles), jnp.sin(angles))


def row_twiddle(spec_re, spec_im, direction):
    my_index = lax.axis_index("ctx")
    devices = lax.axis_size("ctx")
    row_count = spec_re.shape[1]
    period = 2 * devices * row_count
    freq_pair = 2 * my_index + jnp.arange(2, dtype=jnp.int32)
    product = freq_pair[:, None] * jnp.arange(row_count, dtype=jnp.int32)[None, :] % period
    angles = direction * 2.0 * math.pi / period * product.astype(jnp.float32)
    cosine = jnp.cos(angles)[:, :, None]
    sine_part = jnp.sin(angles)[:, :, None]
    return (spec_re * cosine - spec_im * sine_part, spec_re * sine_part + spec_im * cosine)


def row_transform(spec_re, spec_im, direction):
    row_count = spec_re.shape[1]
    cosine, sine_part = angle_table(row_count, row_count, row_count, direction)

    def along_rows(blocks, matrix):
        return jnp.einsum("kmc,mq->kqc", blocks, matrix, precision=highest_precision)

    return (
        along_rows(spec_re, cosine) - along_rows(spec_im, sine_part),
        along_rows(spec_re, sine_part) + along_rows(spec_im, cosine),
    )


def mixing(matrix, blocks):
    return jnp.einsum("kj,jmc->kmc", matrix, blocks, precision=highest_precision)


def forward_spectrum(real_part):
    devices = lax.axis_size("ctx")
    cosine, sine_part = angle_table(2 * devices, devices, 2 * devices, -1.0)
    spread_re = lax.all_to_all(real_part[None], "ctx", split_axis=1, concat_axis=0, tiled=True)
    column_re = mixing(cosine, spread_re)
    column_im = mixing(sine_part, spread_re)
    near_re, near_im = (
        lax.all_to_all(column_re, "ctx", split_axis=0, concat_axis=1, tiled=True),
        lax.all_to_all(column_im, "ctx", split_axis=0, concat_axis=1, tiled=True),
    )
    twist_re, twist_im = row_twiddle(near_re, near_im, -1.0)
    return row_transform(twist_re, twist_im, -1.0)


def inverse_spectrum(spec_re, spec_im):
    devices = lax.axis_size("ctx")
    row_count = spec_re.shape[1]
    back_re, back_im = row_transform(spec_re, spec_im, 1.0)
    twist_re, twist_im = row_twiddle(back_re / row_count, back_im / row_count, 1.0)
    far_re, far_im = (
        lax.all_to_all(twist_re, "ctx", split_axis=1, concat_axis=0, tiled=True),
        lax.all_to_all(twist_im, "ctx", split_axis=1, concat_axis=0, tiled=True),
    )
    cosine, sine_part = angle_table(devices, 2 * devices, 2 * devices, 1.0)
    out_re = (mixing(cosine, far_re) - mixing(sine_part, far_im)) / (2 * devices)
    rows_re = lax.all_to_all(out_re, "ctx", split_axis=0, concat_axis=1, tiled=True)
    return (rows_re[0], rows_re[0])


def pack_columns(values):
    return (values, values)


def by_filter(val_re, val_im, fil_re, fil_im, conjugate):
    val_shape = val_re.shape
    group_count = fil_re.shape[2]
    v_re = val_re.reshape(val_shape[0], val_shape[1], group_count, -1)
    v_im = val_im.reshape(val_shape[0], val_shape[1], group_count, -1)
    f_re = fil_re[:, :, :, None]
    f_im = fil_im[:, :, :, None]
    if conjugate:
        f_im = -f_im
    out_re = v_re * f_re - v_im * f_im
    out_im = v_re * f_im + v_im * f_re
    return (out_re.reshape(val_shape), out_im.reshape(val_shape))


def short_local(extended, filters, seg_ext):
    reach_taps = filters.shape[1]
    out_rows = extended.shape[1] - reach_taps + 1
    own_seg = seg_ext[reach_taps - 1 :]
    running = jnp.zeros((extended.shape[0], out_rows, extended.shape[2]), jnp.float32)
    for shift_by in range(reach_taps):
        start_row = reach_taps - 1 - shift_by
        same_doc = jnp.where(seg_ext[start_row : start_row + out_rows] == own_seg, 1.0, 0.0)
        running = (
            running
            + filters[:, shift_by][:, None, :]
            * same_doc[None, :, None]
            * extended[:, start_row : start_row + out_rows]
        )
    return running


def per_device(projected, segment_ids, short_filter, long_filter, out_proj, mixed_cotangent):
    row_count = projected.shape[2]
    stacked = projected.shape[0]
    width_dev = projected.shape[3]
    short_reach = short_filter.shape[1]
    group_count = long_filter.shape[0]
    grad_scale = 1.0 / math.sqrt(
        projected.shape[1] * lax.axis_size("dp") * row_count * lax.axis_size("ctx")
    )
    segments = segment_ids[0]
    source = projected[:, 0]
    short_rows = short_reach - 1
    cot_full = lax.all_gather(mixed_cotangent[0], "tp", axis=1, tiled=True)
    prev_tail, prev_seg = shifted(
        (source[:, row_count - short_rows :], segments[row_count - short_rows :]), "ctx", 1
    )
    short_seg = jnp.concatenate([prev_seg, segments])
    short_ext = jnp.concatenate([prev_tail, source], axis=1).astype(jnp.float32)

    def short_piece(extended, filters):
        return short_local(extended, filters, short_seg)

    short_out, short_pull = jax.vjp(short_piece, short_ext, short_filter)
    query_conv = short_out[0]
    gated_rows = short_out[1] * short_out[2]
    filter_cols = long_filter.T
    mid_re, mid_im = pack_columns(gated_rows)
    spec_re, spec_im = forward_spectrum(jnp.concatenate([mid_re, filter_cols], axis=1))
    data_cols = spec_re.shape[2] - group_count
    signal_re = spec_re[:, :, :data_cols]
    signal_im = spec_im[:, :, :data_cols]
    filt_re = spec_re[:, :, data_cols:]
    filt_im = spec_im[:, :, data_cols:]
    long_re, long_im = by_filter(signal_re, signal_im, filt_re, filt_im, False)
    out_re, out_im = inverse_spectrum(long_re, long_im)
    y_out = (query_conv * out_re).astype(jnp.bfloat16)
    partial_out = jnp.dot(y_out, out_proj, preferred_element_type=jnp.float32)
    mixed = lax.psum_scatter(partial_out, "tp", scatter_dimension=1, tiled=True).astype(
        jnp.bfloat16
    )
    grad_y = jnp.dot(cot_full, out_proj.T, preferred_element_type=jnp.float32)
    grad_proj_local = jnp.dot(y_out.T, cot_full, preferred_element_type=jnp.float32)
    grad_long_out = grad_y * query_conv
    grad_query = grad_y * out_re
    grad_in_re, grad_in_im = pack_columns(grad_long_out)
    cot_re, cot_im = forward_spectrum(grad_in_re)
    back_re, back_im = by_filter(cot_re, cot_im, filt_re, filt_im, True)
    cross_re = (
        (signal_re * cot_re + signal_im * cot_im).reshape(2, row_count, group_count, -1).sum(axis=3)
    )
    cross_im = (
        (signal_re * cot_im - signal_im * cot_re).reshape(2, row_count, group_count, -1).sum(axis=3)
    )
    inv_re, inv_im = inverse_spectrum(
        jnp.concatenate([back_re, cross_re], axis=2), jnp.concatenate([back_im, cross_im], axis=2)
    )
    grad_gated = inv_re[:, :data_cols]
    grad_long_local = inv_re[:, data_cols:].T
    grad_short_out = jnp.stack([grad_query, grad_gated * short_out[2], grad_gated * short_out[1]])
    grad_short_ext, grad_short_local = short_pull(grad_short_out)
    returned_short = shifted(grad_short_ext[:, :short_rows], "ctx", -1)
    grad_source = grad_short_ext[:, short_rows:] + jnp.concatenate(
        [jnp.zeros((stacked, row_count - short_rows, width_dev), jnp.float32), returned_short],
        axis=1,
    )
    total_proj, total_short = lax.psum((grad_proj_local, grad_short_local), ("ctx", "dp"))
    total_long = lax.psum(grad_long_local, "dp")
    return (
        mixed[None],
        grad_source[:, None].astype(jnp.bfloat16),
        total_short * grad_scale,
        total_long * grad_scale,
        total_proj * grad_scale,
    )


def solution(mesh):
    in_specs = (
        P(None, "dp", "ctx", "tp"),
        P("dp", "ctx"),
        P(None, None, "tp"),
        P("tp", "ctx"),
        P("tp", None),
        P("dp", "ctx", "tp"),
    )
    out_specs = (
        P("dp", "ctx", "tp"),
        P(None, "dp", "ctx", "tp"),
        P(None, None, "tp"),
        P("tp", "ctx"),
        P("tp", None),
    )
    return jax.shard_map(
        per_device, mesh=mesh, in_specs=in_specs, out_specs=out_specs, check_vma=False
    )
```

profile of v0, /device:TPU:7, one launch (start us, length us, event | category | flops | bytes accessed | tf_op | source)
XLA Modules:
  0.0 859.4 jit_solution(18165859684335897357)
XLA Ops:
  8.8 3.2 collective-permute-start.1
  12.7 3.2 collective-permute-start
  16.8 11.0 %all-gather = bf16[1,256,1024]{2,1,0:T(8,128)(2,1)S(1)} all-gather(bf16[1,256,256]{2,1,0:T(8,128)(2,1)} %param.11), channel_id=2, replica_groups=mesh['ctx'=64,'tp'=4,'dp'=2] {'tp'}, dimensions={2}, use_global_device_ids=true | all-gather | bytes 655360 | tf_op jit(solution)/shard_map/all_gather | solution.py:132
  31.3 13.8 %all-to-all-start.6 = ((f32[1,256,256]{2,0,1:T(1,128)}), f32[1,256,256]{2,0,1:T(1,128)S(1)}, u32[]{:S(2)}, u32[]{:S(2)}) async-start(f32[1,256,256]{2,0,1:T(1,128)} %copy.152), calls=%async_computation.7 | async-start | bytes 524288 | tf_op jit(solution)/shard_map/all_to_all | solution.py:59
  46.4 11.2 %all-to-all-done.6 = f32[1,256,256]{2,0,1:T(1,128)S(1)} async-done(((f32[1,256,256]{2,0,1:T(1,128)}), f32[1,256,256]{2,0,1:T(1,128)S(1)}, u32[]{:S(2)}, u32[]{:S(2)}) %all-to-all-start.6) | async-done | bytes 262176 | tf_op jit(solution)/shard_map/all_to_all | solution.py:59
  57.6 4.6 all-to-all-start
  64.9 10.9 %all-to-all-done = f32[1,256,272]{2,0,1:T(1,128)S(1)} async-done(((f32[1,256,272]{2,0,1:T(1,128)}), f32[1,256,272]{2,0,1:T(1,128)S(1)}, u32[]{:S(2)}, u32[]{:S(2)}) %all-to-all-start) | async-done | bytes 278560 | tf_op jit(solution)/shard_map/all_to_all | solution.py:59
  75.7 4.6 all-to-all-start.7
  82.3 12.6 %all-to-all-done.7 = f32[128,4,256]{2,1,0:T(4,128)S(1)} async-done(((f32[128,4,256]{2,1,0:T(4,128)}), f32[128,4,256]{2,1,0:T(4,128)S(1)}, u32[]{:S(2)}, u32[]{:S(2)}) %all-to-all-start.7) | async-done | bytes 524320 | tf_op jit(solution)/shard_map/all_to_all | solution.py:63
  95.7 5.5 all-to-all-start.8
  104.7 10.7 %all-to-all-done.8 = f32[128,4,256]{2,1,0:T(4,128)} async-done(((f32[128,4,256]{2,1,0:T(4,128)}), f32[128,4,256]{2,1,0:T(4,128)}, u32[]{:S(2)}, u32[]{:S(2)}) %all-to-all-start.8) | async-done | bytes 524320 | tf_op jit(solution)/shard_map/all_to_all | solution.py:64
  115.4 5.0 all-to-all-start.1
  124.6 12.5 %all-to-all-done.1 = f32[128,4,272]{2,1,0:T(4,128)S(1)} async-done(((f32[128,4,272]{2,1,0:T(4,128)}), f32[128,4,272]{2,1,0:T(4,128)S(1)}, u32[]{:S(2)}, u32[]{:S(2)}) %all-to-all-start.1) | async-done | bytes 557088 | tf_op jit(solution)/shard_map/all_to_all | solution.py:63
  137.1 5.9 all-to-all-start.2
  150.2 2.7 fusion.42
  164.2 3.5 fusion.52
  167.7 2.4 fusion.45
  171.7 2.7 fusion.3
  188.3 11.5 %all-to-all-start.3 = ((f32[2,256,256]{2,0,1:T(2,128)}), f32[2,256,256]{2,0,1:T(2,128)S(1)}, u32[]{:S(2)}, u32[]{:S(2)}) async-start(f32[2,256,256]{2,0,1:T(2,128)} %copy.147), calls=%async_computation.3 | async-start | bytes 1048576 | tf_op jit(solution)/shard_map/all_to_all | solution.py:76
  201.1 13.1 %all-to-all-done.3 = f32[2,256,256]{2,0,1:T(2,128)S(1)} async-done(((f32[2,256,256]{2,0,1:T(2,128)}), f32[2,256,256]{2,0,1:T(2,128)S(1)}, u32[]{:S(2)}, u32[]{:S(2)}) %all-to-all-start.3) | async-done | bytes 524320 | tf_op jit(solution)/shard_map/all_to_all | solution.py:76
  215.0 5.5 all-to-all-start.4
  228.2 6.5 all-to-all-done.4
  234.7 5.9 all-to-all-start.9
  241.7 15.2 %all-to-all-done.9 = f32[2,256,272]{2,0,1:T(2,128)S(1)} async-done(((f32[2,256,272]{2,0,1:T(2,128)}), f32[2,256,272]{2,0,1:T(2,128)S(1)}, u32[]{:S(2)}, u32[]{:S(2)}) %all-to-all-start.9) | async-done | bytes 557088 | tf_op jit(solution)/shard_map/all_to_all | solution.py:76
  256.9 5.6 all-to-all-start.10
  272.7 6.4 all-to-all-done.10
  279.1 5.6 all-to-all-start.5
  288.6 10.0 %all-to-all-done.5 = f32[64,4,256]{2,1,0:T(4,128)S(1)} async-done(((f32[64,4,256]{2,1,0:T(4,128)}), f32[64,4,256]{2,1,0:T(4,128)S(1)}, u32[]{:S(2)}, u32[]{:S(2)}) %all-to-all-start.5) | async-done | bytes 262176 | tf_op jit(solution)/shard_map/all_to_all | solution.py:81
  298.6 4.6 all-to-all-start.11
  304.1 15.2 %all-to-all-done.11 = f32[64,4,272]{2,1,0:T(4,128)S(1)} async-done(((f32[64,4,272]{2,1,0:T(4,128)}), f32[64,4,272]{2,1,0:T(4,128)S(1)}, u32[]{:S(2)}, u32[]{:S(2)}) %all-to-all-start.11) | async-done | bytes 278560 | tf_op jit(solution)/shard_map/all_to_all | solution.py:81
  327.9 505.0 %psum.21 = f32[3,3,256]{2,0,1:T(4,128)S(1)} all-reduce(f32[3,3,256]{2,0,1:T(4,128)S(1)} %pad_add_fusion.1), channel_id=1, replica_groups=mesh['ctx'=64,'tp'=4,'dp'=2] {'ctx','dp'}, use_global_device_ids=true, to_apply=%region_6.7 | all-reduce | flops 2304 | bytes 18432 | tf_op jit(solution)/shard_map/psum | solution.py:185
  833.9 9.2 %psum.22 = f32[16,256]{0,1:T(8,128)S(1)} all-reduce(f32[16,256]{0,1:T(8,128)S(1)} %slice_bitcast_fusion.3), channel_id=1, replica_groups=mesh['ctx'=64,'tp'=4,'dp'=2] {'dp'}, use_global_device_ids=true, to_apply=%region_7.8 | all-reduce | flops 4096 | bytes 32768 | tf_op jit(solution)/shard_map/psum | solution.py:186
  (163 shorter events, 97.2 us)
Async XLA Ops:
  8.0 19.8 %copy-start = (bf16[256,1024]{1,0:T(8,128)(2,1)S(1)}, bf16[256,1024]{1,0:T(8,128)(2,1)}, u32[]{:S(2)}) copy-start(bf16[256,1024]{1,0:T(8,128)(2,1)} %param.10) | copy-start | bytes 1572868
  8.8 19.8 %collective-permute-start.1 = (s32[2]{0:T(128)S(1)}, s32[2]{0:T(128)S(1)}, u32[]{:S(2)}, u32[]{:S(2)}) collective-permute-start(s32[2]{0:T(128)S(1)} %slice_bitcast_fusion.4), channel_id=1, source_target_pairs={{0,8},{8,16},{16,24},{24,32},{32,40},{40,48},{48,56},{56,64},{64,7... | collective-permute-start | bytes 32 | tf_op jit(solution)/shard_map/ppermute | solution.py:13
  12.7 16.7 %collective-permute-start = (bf16[3,2,256]{2,1,0:T(2,128)(2,1)S(1)}, bf16[3,2,256]{2,1,0:T(2,128)(2,1)S(1)}, u32[]{:S(2)}, u32[]{:S(2)}) collective-permute-start(bf16[3,2,256]{2,1,0:T(2,128)(2,1)S(1)} %slice.90), channel_id=1, source_target_pairs={{0,8},{8,16},{16,24},{24,32},{32,40},{40,48},{48,56},{56,64},{64,7... | collective-permute-start | bytes 9224 | tf_op jit(solution)/shard_map/ppermute | solution.py:13
  28.6 1.7 copy-start.8
  31.3 13.8 %copy-start.27 = (f32[16,256]{1,0:T(8,128)S(1)}, f32[16,256]{1,0:T(8,128)}, u32[]{:S(2)}) copy-start(f32[16,256]{1,0:T(8,128)} %param.9) | copy-start | bytes 49156
  31.3 26.3 %all-to-all-start.6 = ((f32[1,256,256]{2,0,1:T(1,128)}), f32[1,256,256]{2,0,1:T(1,128)S(1)}, u32[]{:S(2)}, u32[]{:S(2)}) async-start(f32[1,256,256]{2,0,1:T(1,128)} %copy.152), calls=%async_computation.7 | async-start | bytes 524288 | tf_op jit(solution)/shard_map/all_to_all | solution.py:59
  57.6 18.1 %all-to-all-start = ((f32[1,256,272]{2,0,1:T(1,128)}), f32[1,256,272]{2,0,1:T(1,128)S(1)}, u32[]{:S(2)}, u32[]{:S(2)}) async-start(f32[1,256,272]{2,0,1:T(1,128)} %copy.126), calls=%async_computation | async-start | bytes 786432 | tf_op jit(solution)/shard_map/all_to_all | solution.py:59
  75.7 19.2 %all-to-all-start.7 = ((f32[128,4,256]{2,1,0:T(4,128)}), f32[128,4,256]{2,1,0:T(4,128)S(1)}, u32[]{:S(2)}, u32[]{:S(2)}) async-start(f32[128,4,256]{2,1,0:T(4,128)} %copy.154), calls=%async_computation.8 | async-start | bytes 1048576 | tf_op jit(solution)/shard_map/all_to_all | solution.py:63
  95.7 19.7 %all-to-all-start.8 = ((f32[128,4,256]{2,1,0:T(4,128)}), f32[128,4,256]{2,1,0:T(4,128)}, u32[]{:S(2)}, u32[]{:S(2)}) async-start(f32[128,4,256]{2,1,0:T(4,128)} %copy.158), calls=%async_computation.9 | async-start | bytes 1048576 | tf_op jit(solution)/shard_map/all_to_all | solution.py:64
  115.4 21.7 %all-to-all-start.1 = ((f32[128,4,272]{2,1,0:T(4,128)}), f32[128,4,272]{2,1,0:T(4,128)S(1)}, u32[]{:S(2)}, u32[]{:S(2)}) async-start(f32[128,4,272]{2,1,0:T(4,128)} %copy.128), calls=%async_computation.1 | async-start | bytes 1572864 | tf_op jit(solution)/shard_map/all_to_all | solution.py:63
  137.1 7.6 copy-start.12
  137.1 22.4 %all-to-all-start.2 = ((f32[128,4,272]{2,1,0:T(4,128)}), f32[128,4,272]{2,1,0:T(4,128)}, u32[]{:S(2)}, u32[]{:S(2)}) async-start(f32[128,4,272]{2,1,0:T(4,128)} %copy.132), calls=%async_computation.2 | async-start | bytes 1572864 | tf_op jit(solution)/shard_map/all_to_all | solution.py:64
  150.2 2.7 copy-start.24
  159.5 1.7 copy-start.20
  164.2 3.5 copy-start.22
  171.6 2.7 copy-start.21
  174.4 1.7 copy-start.5
  174.4 1.7 copy-start.23
  188.3 25.9 %all-to-all-start.3 = ((f32[2,256,256]{2,0,1:T(2,128)}), f32[2,256,256]{2,0,1:T(2,128)S(1)}, u32[]{:S(2)}, u32[]{:S(2)}) async-start(f32[2,256,256]{2,0,1:T(2,128)} %copy.147), calls=%async_computation.3 | async-start | bytes 1048576 | tf_op jit(solution)/shard_map/all_to_all | solution.py:76
  201.1 19.4 %copy-start.25 = (f32[2,256,256]{1,2,0:T(8,128)S(1)}, f32[2,256,256]{1,2,0:T(8,128)}, u32[]{:S(2)}) copy-start(f32[2,256,256]{1,2,0:T(8,128)} %get-tuple-element.41) | copy-start | bytes 1572868
  215.0 19.7 %all-to-all-start.4 = ((f32[2,256,256]{2,0,1:T(2,128)}), f32[2,256,256]{2,0,1:T(2,128)}, u32[]{:S(2)}, u32[]{:S(2)}) async-start(f32[2,256,256]{2,0,1:T(2,128)} %copy.149), calls=%async_computation.4 | async-start | bytes 1048576 | tf_op jit(solution)/shard_map/all_to_all | solution.py:77
  234.7 22.2 %all-to-all-start.9 = ((f32[2,256,272]{2,0,1:T(2,128)}), f32[2,256,272]{2,0,1:T(2,128)S(1)}, u32[]{:S(2)}, u32[]{:S(2)}) async-start(f32[2,256,272]{2,0,1:T(2,128)} %copy.165), calls=%async_computation.10 | async-start | bytes 1572864 | tf_op jit(solution)/shard_map/all_to_all | solution.py:76
  241.7 20.8 %copy-start.14 = (f32[2,256,256]{2,0,1:T(2,128)S(1)}, f32[2,256,256]{2,0,1:T(2,128)}, u32[]{:S(2)}) copy-start(f32[2,256,256]{2,0,1:T(2,128)} %copy-done.13) | copy-start | bytes 1572868
  256.9 22.2 %all-to-all-start.10 = ((f32[2,256,272]{2,0,1:T(2,128)}), f32[2,256,272]{2,0,1:T(2,128)}, u32[]{:S(2)}, u32[]{:S(2)}) async-start(f32[2,256,272]{2,0,1:T(2,128)} %copy.168), calls=%async_computation.11 | async-start | bytes 1572864 | tf_op jit(solution)/shard_map/all_to_all | solution.py:77
  279.1 19.5 %all-to-all-start.5 = ((f32[64,4,256]{2,1,0:T(4,128)}), f32[64,4,256]{2,1,0:T(4,128)S(1)}, u32[]{:S(2)}, u32[]{:S(2)}) async-start(f32[64,4,256]{2,1,0:T(4,128)} %copy.151), calls=%async_computation.5 | async-start | bytes 524288 | tf_op jit(solution)/shard_map/all_to_all | solution.py:81
  298.6 20.7 %all-to-all-start.11 = ((f32[64,4,272]{2,1,0:T(4,128)}), f32[64,4,272]{2,1,0:T(4,128)S(1)}, u32[]{:S(2)}, u32[]{:S(2)}) async-start(f32[64,4,272]{2,1,0:T(4,128)} %copy.171), calls=%async_computation.12 | async-start | bytes 786432 | tf_op jit(solution)/shard_map/all_to_all | solution.py:81
  303.2 544.3 %all-reduce.9.cloned.1.call-start = ((), (), s32[]{:S(2)}) async-start(), calls=%async_computation.14 | async-start | bytes 2097152 | tf_op jit(solution)/shard_map/psum | solution.py:185
  304.1 16.1 %copy-start.9 = (f32[256,256]{1,0:T(8,128)S(1)}, f32[256,256]{1,0:T(8,128)}, u32[]{:S(2)}) copy-start(f32[256,256]{1,0:T(8,128)} %copy-done.8) | copy-start | bytes 786436
  321.5 2.7 copy-start.10
  322.8 527.1 %reduce-scatter.2.cloned.1.call-start = ((), (), s32[]{:S(2)}) async-start(), calls=%async_computation.13 | async-start | bytes 1310720 | tf_op jit(solution)/shard_map/reduce_scatter | solution.py:157
  326.5 516.7 %copy-start.2 = (f32[3,256,256]{2,1,0:T(8,128)S(1)}, f32[3,256,256]{2,1,0:T(8,128)}, u32[]{:S(2)}) copy-start(f32[3,256,256]{2,1,0:T(8,128)} %copy-done.1) | copy-start | bytes 2359300
  326.5 519.1 %collective-permute-start.2 = (f32[3,2,256]{2,1,0:T(2,128)S(1)}, f32[3,2,256]{2,1,0:T(2,128)S(1)}, u32[]{:S(2)}, u32[]{:S(2)}) collective-permute-start(f32[3,2,256]{2,1,0:T(2,128)S(1)} %pad_add_fusion.2), channel_id=1, source_target_pairs={{8,0},{16,8},{24,16},{32,24},{40,32},{48,40},{56,48},{64,56},{72,6... | collective-permute-start | bytes 18440 | tf_op jit(solution)/shard_map/ppermute | solution.py:13
  (16 other events, 18.9 us)
Sparse Core Ops, SparseCore 0:
  322.9 206.9 all-reduce.8
Sparse Core Ops, SparseCore 1:
  326.1 37.0 reduce-scatter.1
where the time goes:
time: 870 us; the launch traced here: 859 us
  blocking collectives  525 us (60%)
  waiting for transfers between devices  125 us (14%)
  starting transfers between devices  86 us (10%)
  local copies, waits for them, and re-layouts  45.5 us (5%)
  matrix products  44.1 us (5%)
  other arithmetic  16.9 us (2%)
  between operations  16.7 us (2%)
    psum x1, blocking collectives, per_device(): lax.psum((grad_proj_local, grad_short_local), ('ctx', 'dp'))  505 us
    dot_general x16, matrix products, along_rows(): jnp.einsum('kmc,mq->kqc', blocks, matrix, precision=highest_precision)  34.1 us
    all_to_all x2, waiting for transfers between devices, inverse_spectrum(): lax.all_to_all(twist_re, 'ctx', split_axis=1, concat_axis=0, tiled=True)  28.3 us
    all_to_all x2, waiting for transfers between devices, inverse_spectrum(): lax.all_to_all(out_re, 'ctx', split_axis=0, concat_axis=1, tiled=True)  25.3 us
    all_to_all x2, waiting for transfers between devices, forward_spectrum(): lax.all_to_all(column_re, 'ctx', split_axis=0, concat_axis=1, tiled=True)  25.1 us
    all_to_all x2, waiting for transfers between devices, forward_spectrum(): lax.all_to_all(real_part[None], 'ctx', split_axis=1, concat_axis=0, tiled...  22.1 us
    all_to_all x2, starting transfers between devices, forward_spectrum(): lax.all_to_all(real_part[None], 'ctx', split_axis=1, concat_axis=0, tiled...  18.4 us
    all_to_all x2, starting transfers between devices, inverse_spectrum(): lax.all_to_all(twist_re, 'ctx', split_axis=1, concat_axis=0, tiled=True)  17.4 us
  transfers between devices with their start and end apart: 17, of which 12 were waited for; matrix products, arithmetic and copies ran while one was open for 7% of the time, Pallas kernels for 0%

commit v1 on v0

--- a/solution.py
+++ b/solution.py
@@ -5,6 +5,7 @@
 from jax.sharding import PartitionSpec as P
 
 highest_precision = lax.Precision.HIGHEST
+put_packet = lambda x_part: lax.psum(lax.psum(x_part, "dp"), "ctx")
 
 
 def shifted(value, axis, steps):
@@ -182,7 +183,7 @@
         [jnp.zeros((stacked, row_count - short_rows, width_dev), jnp.float32), returned_short],
         axis=1,
     )
-    total_proj, total_short = lax.psum((grad_proj_local, grad_short_local), ("ctx", "dp"))
+    total_proj, total_short = put_packet((grad_proj_local, grad_short_local))
     total_long = lax.psum(grad_long_local, "dp")
     return (
         mixed[None],

time: 870 us -> 811 us (0.932)
  blocking collectives: 525 us -> 256 us
  waiting for transfers between devices: 125 us -> 322 us
    psum x2, blocking collectives: 514 us -> 245 us  [put_packet = lambda x_part: lax.psum(lax.psum(x_part, 'dp'), 'ctx')]
    psum x1 -> x2, waiting for transfers between devices: 0.01 us -> 198 us  [put_packet = lambda x_part: lax.psum(lax.psum(x_part, 'dp'), 'ctx')]
  transfers between devices with their start and end apart: 17 -> 18, of which waited for: 12 -> 12; matrix products, arithmetic and copies ran while one was open for 7% -> 8% of each run, Pallas kernels for 0% -> 0%
where the time goes in v1:
time: 811 us; the launch traced here: 797 us
  waiting for transfers between devices  322 us (40%)
  blocking collectives  256 us (32%)
  starting transfers between devices  86.3 us (11%)
  local copies, waits for them, and re-layouts  54 us (7%)
  matrix products  44.2 us (5%)
  other arithmetic  16.9 us (2%)
  between operations  16.7 us (2%)
    psum x2, blocking collectives, put_packet = lambda x_part: lax.psum(lax.psum(x_part, 'dp'), 'ctx')  245 us
    psum x2, waiting for transfers between devices, put_packet = lambda x_part: lax.psum(lax.psum(x_part, 'dp'), 'ctx')  198 us
    dot_general x16, matrix products, along_rows(): jnp.einsum('kmc,mq->kqc', blocks, matrix, precision=highest_precision)  34.1 us
    all_to_all x2, waiting for transfers between devices, inverse_spectrum(): lax.all_to_all(twist_re, 'ctx', split_axis=1, concat_axis=0, tiled=True)  28.3 us
    all_to_all x2, waiting for transfers between devices, inverse_spectrum(): lax.all_to_all(out_re, 'ctx', split_axis=0, concat_axis=1, tiled=True)  25.3 us
    all_to_all x2, waiting for transfers between devices, forward_spectrum(): lax.all_to_all(column_re, 'ctx', split_axis=0, concat_axis=1, tiled=True)  25.1 us
    all_to_all x2, waiting for transfers between devices, forward_spectrum(): lax.all_to_all(real_part[None], 'ctx', split_axis=1, concat_axis=0, tiled...  22.1 us
    all_to_all x2, starting transfers between devices, forward_spectrum(): lax.all_to_all(real_part[None], 'ctx', split_axis=1, concat_axis=0, tiled...  18.4 us
  transfers between devices with their start and end apart: 18, of which 12 were waited for; matrix products, arithmetic and copies ran while one was open for 8% of the time, Pallas kernels for 0%

profile of v1, /device:TPU:7, one launch (start us, length us, event | category | flops | bytes accessed | tf_op | source)
XLA Modules:
  0.0 796.8 jit_solution(13303643139567577864)
XLA Ops:
  8.8 3.2 collective-permute-start.1
  12.7 3.2 collective-permute-start
  16.8 11.0 %all-gather = bf16[1,256,1024]{2,1,0:T(8,128)(2,1)S(1)} all-gather(bf16[1,256,256]{2,1,0:T(8,128)(2,1)} %param.11), channel_id=2, replica_groups=mesh['ctx'=64,'tp'=4,'dp'=2] {'tp'}, dimensions={2}, use_global_device_ids=true | all-gather | bytes 655360 | tf_op jit(solution)/shard_map/all_gather | solution.py:133
  30.9 13.8 %all-to-all-start.6 = ((f32[1,256,256]{2,0,1:T(1,128)}), f32[1,256,256]{2,0,1:T(1,128)S(1)}, u32[]{:S(2)}, u32[]{:S(2)}) async-start(f32[1,256,256]{2,0,1:T(1,128)} %copy.152), calls=%async_computation.7 | async-start | bytes 524288 | tf_op jit(solution)/shard_map/all_to_all | solution.py:60
  46.0 11.2 %all-to-all-done.6 = f32[1,256,256]{2,0,1:T(1,128)S(1)} async-done(((f32[1,256,256]{2,0,1:T(1,128)}), f32[1,256,256]{2,0,1:T(1,128)S(1)}, u32[]{:S(2)}, u32[]{:S(2)}) %all-to-all-start.6) | async-done | bytes 262176 | tf_op jit(solution)/shard_map/all_to_all | solution.py:60
  57.2 4.6 all-to-all-start
  64.4 10.9 %all-to-all-done = f32[1,256,272]{2,0,1:T(1,128)S(1)} async-done(((f32[1,256,272]{2,0,1:T(1,128)}), f32[1,256,272]{2,0,1:T(1,128)S(1)}, u32[]{:S(2)}, u32[]{:S(2)}) %all-to-all-start) | async-done | bytes 278560 | tf_op jit(solution)/shard_map/all_to_all | solution.py:60
  75.3 4.6 all-to-all-start.7
  81.8 12.6 %all-to-all-done.7 = f32[128,4,256]{2,1,0:T(4,128)S(1)} async-done(((f32[128,4,256]{2,1,0:T(4,128)}), f32[128,4,256]{2,1,0:T(4,128)S(1)}, u32[]{:S(2)}, u32[]{:S(2)}) %all-to-all-start.7) | async-done | bytes 524320 | tf_op jit(solution)/shard_map/all_to_all | solution.py:64
  95.3 5.5 all-to-all-start.8
  104.2 10.7 %all-to-all-done.8 = f32[128,4,256]{2,1,0:T(4,128)} async-done(((f32[128,4,256]{2,1,0:T(4,128)}), f32[128,4,256]{2,1,0:T(4,128)}, u32[]{:S(2)}, u32[]{:S(2)}) %all-to-all-start.8) | async-done | bytes 524320 | tf_op jit(solution)/shard_map/all_to_all | solution.py:65
  114.9 4.9 all-to-all-start.1
  124.1 12.5 %all-to-all-done.1 = f32[128,4,272]{2,1,0:T(4,128)S(1)} async-done(((f32[128,4,272]{2,1,0:T(4,128)}), f32[128,4,272]{2,1,0:T(4,128)S(1)}, u32[]{:S(2)}, u32[]{:S(2)}) %all-to-all-start.1) | async-done | bytes 557088 | tf_op jit(solution)/shard_map/all_to_all | solution.py:64
  136.6 5.8 all-to-all-start.2
  164.3 3.6 fusion.52
  170.2 10.1 %copy.136 = f32[2,256,272]{1,2,0:T(8,128)S(1)} copy(f32[2,256,272]{2,0,1:T(2,128)} %get-tuple-element.32) | data formatting | bytes 1114112 | tf_op jit(solution)/shard_map/add | solution.py:37
  180.3 2.7 fusion.3
  197.0 12.1 %all-to-all-start.3 = ((f32[2,256,256]{2,0,1:T(2,128)}), f32[2,256,256]{2,0,1:T(2,128)S(1)}, u32[]{:S(2)}, u32[]{:S(2)}) async-start(f32[2,256,256]{2,0,1:T(2,128)} %copy.147), calls=%async_computation.3 | async-start | bytes 1048576 | tf_op jit(solution)/shard_map/all_to_all | solution.py:77
  210.3 13.1 %all-to-all-done.3 = f32[2,256,256]{2,0,1:T(2,128)S(1)} async-done(((f32[2,256,256]{2,0,1:T(2,128)}), f32[2,256,256]{2,0,1:T(2,128)S(1)}, u32[]{:S(2)}, u32[]{:S(2)}) %all-to-all-start.3) | async-done | bytes 524320 | tf_op jit(solution)/shard_map/all_to_all | solution.py:77
  224.2 5.5 all-to-all-start.4
  237.5 6.5 all-to-all-done.4
  243.9 5.9 all-to-all-start.9
  251.0 15.2 %all-to-all-done.9 = f32[2,256,272]{2,0,1:T(2,128)S(1)} async-done(((f32[2,256,272]{2,0,1:T(2,128)}), f32[2,256,272]{2,0,1:T(2,128)S(1)}, u32[]{:S(2)}, u32[]{:S(2)}) %all-to-all-start.9) | async-done | bytes 557088 | tf_op jit(solution)/shard_map/all_to_all | solution.py:77
  266.2 5.6 all-to-all-start.10
  281.9 6.5 all-to-all-done.10
  288.4 5.6 all-to-all-start.5
  297.8 10.1 %all-to-all-done.5 = f32[64,4,256]{2,1,0:T(4,128)S(1)} async-done(((f32[64,4,256]{2,1,0:T(4,128)}), f32[64,4,256]{2,1,0:T(4,128)S(1)}, u32[]{:S(2)}, u32[]{:S(2)}) %all-to-all-start.5) | async-done | bytes 262176 | tf_op jit(solution)/shard_map/all_to_all | solution.py:82
  307.9 4.6 all-to-all-start.11
  313.4 15.2 %all-to-all-done.11 = f32[64,4,272]{2,1,0:T(4,128)S(1)} async-done(((f32[64,4,272]{2,1,0:T(4,128)}), f32[64,4,272]{2,1,0:T(4,128)S(1)}, u32[]{:S(2)}, u32[]{:S(2)}) %all-to-all-start.11) | async-done | bytes 278560 | tf_op jit(solution)/shard_map/all_to_all | solution.py:82
  337.4 23.5 %all-reduce.7 = (f32[3,3,256]{2,0,1:T(4,128)S(1)}, f32[16,256]{0,1:T(8,128)S(1)}) all-reduce(f32[3,3,256]{2,0,1:T(4,128)S(1)} %pad_add_fusion.1, f32[16,256]{0,1:T(8,128)S(1)} %slice_bitcast_fusion.3), channel_id=1, replica_groups=mesh['ctx'=64,'tp'=4,'dp'=2] {'dp'}, use_global_device_ids=true, to_apply=%region_6.7 | all-reduce | flops 6400 | bytes 51200 | tf_op jit(solution)/shard_map/psum | solution.py:8
  360.9 221.8 %psum.36 = f32[3,3,256]{2,0,1:T(4,128)S(1)} all-reduce(f32[3,3,256]{2,0,1:T(4,128)S(1)} %get-tuple-element.30), channel_id=1, replica_groups=mesh['ctx'=64,'tp'=4,'dp'=2] {'ctx'}, use_global_device_ids=true, to_apply=%region_7.8 | all-reduce | flops 2304 | bytes 18432 | tf_op jit(solution)/shard_map/psum | solution.py:8
  588.8 197.8 %all-reduce.13.cloned.1.call-done = f32[256,1024]{1,0:T(8,128)} async-done(((f32[256,1024]{1,0:T(8,128)}), f32[256,1024]{1,0:T(8,128)}) %all-reduce.13.cloned.1.call-update) | async-done | bytes 1048592 | tf_op jit(solution)/shard_map/psum | solution.py:8
  (162 shorter events, 100.3 us)
Async XLA Ops:
  8.0 19.8 %copy-start = (bf16[256,1024]{1,0:T(8,128)(2,1)S(1)}, bf16[256,1024]{1,0:T(8,128)(2,1)}, u32[]{:S(2)}) copy-start(bf16[256,1024]{1,0:T(8,128)(2,1)} %param.10) | copy-start | bytes 1572868
  8.8 19.8 %collective-permute-start.1 = (s32[2]{0:T(128)S(1)}, s32[2]{0:T(128)S(1)}, u32[]{:S(2)}, u32[]{:S(2)}) collective-permute-start(s32[2]{0:T(128)S(1)} %slice_bitcast_fusion.4), channel_id=1, source_target_pairs={{0,8},{8,16},{16,24},{24,32},{32,40},{40,48},{48,56},{56,64},{64,7... | collective-permute-start | bytes 32 | tf_op jit(solution)/shard_map/ppermute | solution.py:14
  12.7 16.7 %collective-permute-start = (bf16[3,2,256]{2,1,0:T(2,128)(2,1)S(1)}, bf16[3,2,256]{2,1,0:T(2,128)(2,1)S(1)}, u32[]{:S(2)}, u32[]{:S(2)}) collective-permute-start(bf16[3,2,256]{2,1,0:T(2,128)(2,1)S(1)} %slice.90), channel_id=1, source_target_pairs={{0,8},{8,16},{16,24},{24,32},{32,40},{40,48},{48,56},{56,64},{64,7... | collective-permute-start | bytes 9224 | tf_op jit(solution)/shard_map/ppermute | solution.py:14
  30.9 13.8 %copy-start.27 = (f32[16,256]{1,0:T(8,128)S(1)}, f32[16,256]{1,0:T(8,128)}, u32[]{:S(2)}) copy-start(f32[16,256]{1,0:T(8,128)} %param.9) | copy-start | bytes 49156
  30.9 26.3 %all-to-all-start.6 = ((f32[1,256,256]{2,0,1:T(1,128)}), f32[1,256,256]{2,0,1:T(1,128)S(1)}, u32[]{:S(2)}, u32[]{:S(2)}) async-start(f32[1,256,256]{2,0,1:T(1,128)} %copy.152), calls=%async_computation.7 | async-start | bytes 524288 | tf_op jit(solution)/shard_map/all_to_all | solution.py:60
  57.2 18.1 %all-to-all-start = ((f32[1,256,272]{2,0,1:T(1,128)}), f32[1,256,272]{2,0,1:T(1,128)S(1)}, u32[]{:S(2)}, u32[]{:S(2)}) async-start(f32[1,256,272]{2,0,1:T(1,128)} %copy.126), calls=%async_computation | async-start | bytes 786432 | tf_op jit(solution)/shard_map/all_to_all | solution.py:60
  75.3 19.2 %all-to-all-start.7 = ((f32[128,4,256]{2,1,0:T(4,128)}), f32[128,4,256]{2,1,0:T(4,128)S(1)}, u32[]{:S(2)}, u32[]{:S(2)}) async-start(f32[128,4,256]{2,1,0:T(4,128)} %copy.154), calls=%async_computation.8 | async-start | bytes 1048576 | tf_op jit(solution)/shard_map/all_to_all | solution.py:64
  95.3 19.7 %all-to-all-start.8 = ((f32[128,4,256]{2,1,0:T(4,128)}), f32[128,4,256]{2,1,0:T(4,128)}, u32[]{:S(2)}, u32[]{:S(2)}) async-start(f32[128,4,256]{2,1,0:T(4,128)} %copy.158), calls=%async_computation.9 | async-start | bytes 1048576 | tf_op jit(solution)/shard_map/all_to_all | solution.py:65
  114.9 21.7 %all-to-all-start.1 = ((f32[128,4,272]{2,1,0:T(4,128)}), f32[128,4,272]{2,1,0:T(4,128)S(1)}, u32[]{:S(2)}, u32[]{:S(2)}) async-start(f32[128,4,272]{2,1,0:T(4,128)} %copy.128), calls=%async_computation.1 | async-start | bytes 1572864 | tf_op jit(solution)/shard_map/all_to_all | solution.py:64
  136.6 7.6 copy-start.12
  136.6 23.0 %all-to-all-start.2 = ((f32[128,4,272]{2,1,0:T(4,128)}), f32[128,4,272]{2,1,0:T(4,128)}, u32[]{:S(2)}, u32[]{:S(2)}) async-start(f32[128,4,272]{2,1,0:T(4,128)} %copy.132), calls=%async_computation.2 | async-start | bytes 1572864 | tf_op jit(solution)/shard_map/all_to_all | solution.py:65
  150.8 2.7 copy-start.24
  159.6 1.7 copy-start.20
  164.3 3.6 copy-start.22
  180.3 2.7 copy-start.21
  183.1 1.7 copy-start.5
  183.1 1.7 copy-start.23
  197.0 26.4 %all-to-all-start.3 = ((f32[2,256,256]{2,0,1:T(2,128)}), f32[2,256,256]{2,0,1:T(2,128)S(1)}, u32[]{:S(2)}, u32[]{:S(2)}) async-start(f32[2,256,256]{2,0,1:T(2,128)} %copy.147), calls=%async_computation.3 | async-start | bytes 1048576 | tf_op jit(solution)/shard_map/all_to_all | solution.py:77
  210.3 19.4 %copy-start.25 = (f32[2,256,256]{1,2,0:T(8,128)S(1)}, f32[2,256,256]{1,2,0:T(8,128)}, u32[]{:S(2)}) copy-start(f32[2,256,256]{1,2,0:T(8,128)} %get-tuple-element.43) | copy-start | bytes 1572868
  224.2 19.7 %all-to-all-start.4 = ((f32[2,256,256]{2,0,1:T(2,128)}), f32[2,256,256]{2,0,1:T(2,128)}, u32[]{:S(2)}, u32[]{:S(2)}) async-start(f32[2,256,256]{2,0,1:T(2,128)} %copy.149), calls=%async_computation.4 | async-start | bytes 1048576 | tf_op jit(solution)/shard_map/all_to_all | solution.py:78
  243.9 22.3 %all-to-all-start.9 = ((f32[2,256,272]{2,0,1:T(2,128)}), f32[2,256,272]{2,0,1:T(2,128)S(1)}, u32[]{:S(2)}, u32[]{:S(2)}) async-start(f32[2,256,272]{2,0,1:T(2,128)} %copy.165), calls=%async_computation.10 | async-start | bytes 1572864 | tf_op jit(solution)/shard_map/all_to_all | solution.py:77
  251.0 20.8 %copy-start.14 = (f32[2,256,256]{2,0,1:T(2,128)S(1)}, f32[2,256,256]{2,0,1:T(2,128)}, u32[]{:S(2)}) copy-start(f32[2,256,256]{2,0,1:T(2,128)} %copy-done.13) | copy-start | bytes 1572868
  266.2 22.2 %all-to-all-start.10 = ((f32[2,256,272]{2,0,1:T(2,128)}), f32[2,256,272]{2,0,1:T(2,128)}, u32[]{:S(2)}, u32[]{:S(2)}) async-start(f32[2,256,272]{2,0,1:T(2,128)} %copy.168), calls=%async_computation.11 | async-start | bytes 1572864 | tf_op jit(solution)/shard_map/all_to_all | solution.py:78
  288.4 19.5 %all-to-all-start.5 = ((f32[64,4,256]{2,1,0:T(4,128)}), f32[64,4,256]{2,1,0:T(4,128)S(1)}, u32[]{:S(2)}, u32[]{:S(2)}) async-start(f32[64,4,256]{2,1,0:T(4,128)} %copy.151), calls=%async_computation.5 | async-start | bytes 524288 | tf_op jit(solution)/shard_map/all_to_all | solution.py:82
  307.9 20.7 %all-to-all-start.11 = ((f32[64,4,272]{2,1,0:T(4,128)}), f32[64,4,272]{2,1,0:T(4,128)S(1)}, u32[]{:S(2)}, u32[]{:S(2)}) async-start(f32[64,4,272]{2,1,0:T(4,128)} %copy.171), calls=%async_computation.12 | async-start | bytes 786432 | tf_op jit(solution)/shard_map/all_to_all | solution.py:82
  312.6 270.2 %all-reduce.11.cloned.1.call-start = ((), (), s32[]{:S(2)}) async-start(), calls=%async_computation.14 | async-start | bytes 2097152 | tf_op jit(solution)/shard_map/psum | solution.py:8
  313.4 16.1 %copy-start.9 = (f32[256,256]{1,0:T(8,128)S(1)}, f32[256,256]{1,0:T(8,128)}, u32[]{:S(2)}) copy-start(f32[256,256]{1,0:T(8,128)} %copy-done.8) | copy-start | bytes 786436
  330.7 2.7 copy-start.10
  332.1 255.1 %reduce-scatter.2.cloned.1.call-start = ((), (), s32[]{:S(2)}) async-start(), calls=%async_computation.13 | async-start | bytes 1310720 | tf_op jit(solution)/shard_map/reduce_scatter | solution.py:158
  333.4 453.2 %all-reduce.13.cloned.1.call-start = ((), (), s32[]{:S(2)}) async-start(), calls=%async_computation.15 | async-start | bytes 2097152 | tf_op jit(solution)/shard_map/psum | solution.py:8
  335.2 250.0 %collective-permute-start.2 = (f32[3,2,256]{2,1,0:T(2,128)S(1)}, f32[3,2,256]{2,1,0:T(2,128)S(1)}, u32[]{:S(2)}, u32[]{:S(2)}) collective-permute-start(f32[3,2,256]{2,1,0:T(2,128)S(1)} %pad_add_fusion.2), channel_id=1, source_target_pairs={{8,0},{16,8},{24,16},{32,24},{40,32},{48,40},{56,48},{64,56},{72,6... | collective-permute-start | bytes 18440 | tf_op jit(solution)/shard_map/ppermute | solution.py:14
  337.4 245.4 %copy-start.2 = (f32[3,256,256]{2,1,0:T(8,128)S(1)}, f32[3,256,256]{2,1,0:T(8,128)}, u32[]{:S(2)}) copy-start(f32[3,256,256]{2,1,0:T(8,128)} %copy-done.1) | copy-start | bytes 2359300
  (15 other events, 19.0 us)
Sparse Core Ops, SparseCore 0:
  332.2 47.8 all-reduce.10
  582.9 203.6 all-reduce.12
Sparse Core Ops, SparseCore 1:
  335.9 37.0 reduce-scatter.1
